TPU v7x, 32 devices: a whole 2x2x4 slice. The times are simulated.
32 devices in a mesh: region: 2 (over y), space: 8 (over z, x), day: 2 (over core).
Axes of the slice: x: 2, y: 2, z: 4, core: 2. Of those that a mesh axis runs over, the one named last changes fastest.
Arguments:
- observed: float32 [4, 64, 4096], P('day', ('region', 'space')), parts along dimension 1, may hold values from -20 to 20
- gap_mask: int32 [4, 64, 4096], P('day', ('region', 'space')), parts along dimension 1, may hold values 0 or 1
- sea_mask: int32 [64, 4096], P(('region', 'space')), parts along dimension 0, may hold values 0 or 1
- stencil: bfloat16 [9, 64, 4096], P(None, ('region', 'space')), parts along dimension 1, may hold values from 0.019897461 to 0.19921875
- precision: float32 [64, 4096], P(('region', 'space')), parts along dimension 0, may hold values from 0.5 to 4
- noise_precision: float32 [64, 4096], P(('region', 'space')), parts along dimension 0, may hold values from 0.5 to 8
- perturbation: bfloat16 [2, 4, 64, 4096], P(None, 'day', ('region', 'space')), parts along dimension 2, may hold values from -6 to 6
Outputs:
- posterior_mean: float32 [4, 64, 4096], P('day', ('region', 'space')), parts along dimension 1
- fitted: float32 [2, 64, 4096], P(None, ('region', 'space'), 'day'), parts along dimension 1
There are 2 independent parts, one for each index of `region`. A program takes and returns all parts, laid end to end along the dimension named above; each array names one. Nothing has to cross between parts.
All inputs are finite; a program needn't handle non-finite values. No bound on the sum of `gap_mask` or of `sea_mask` on one device may be relied on, other than what follows from the above.
Results may differ from a plain program's by a relative error of at most 0.0003.
Values sent between devices are 32-bit elements; how exact they have to be, the bound alone decides.
No kernel may reach another device: no remote copies, remote signals or barrier semaphores. Data moves between devices by JAX's collectives and lax.ppermute only.
A program may use at most 64 MiB of HBM per device.

v0:
```python
import jax
import jax.numpy as jnp
from jax import lax
from jax.sharding import PartitionSpec as P

ITERS = 2
OFFSETS = ((-1, -1), (-1, 0), (-1, 1), (0, -1), (0, 0), (0, 1), (1, -1), (1, 0), (1, 1))
RIDGE = 1.0


def padded(x, sides, width):
    for axis, dim in sides:
        size, length = (lax.axis_size(axis), x.shape[dim])
        up = [(i, (i + 1) % size) for i in range(size - 1)]
        down = [(j, i) for i, j in up]
        last = lax.slice_in_dim(x, length - width, length, axis=dim)
        first = lax.slice_in_dim(x, 0, width, axis=dim)
        before = lax.ppermute(last, axis, up)
        after = lax.ppermute(first, axis, down)
        x = jnp.concatenate([before, x, after], axis=dim)
    return x


def from_behind(x, axis, by):
    size = lax.axis_size(axis)
    pairs = [(i, i + by) for i in range(size) if 0 <= i + by < size]
    return lax.ppermute(x, axis, pairs)


def column_shift(values, col_step):
    if col_step == 0:
        return values
    zero_column = jnp.zeros_like(values[..., :1])
    if col_step > 0:
        return jnp.concatenate([values[..., 1:], zero_column], -1)
    return jnp.concatenate([zero_column, values[..., :-1]], -1)


def forward_rows(values, coefficients):
    height = coefficients.shape[1]
    result = jnp.zeros(values[..., 1:-1, :].shape, jnp.float32)
    for position, (row_step, col_step) in enumerate(OFFSETS):
        rows_taken = values[..., 1 + row_step : 1 + row_step + height, :]
        result = result + coefficients[position] * column_shift(rows_taken, col_step)
    return result


def transposed_rows(values, coefficients):
    height = values.shape[-2] - 2
    result = jnp.zeros(values[..., 1:-1, :].shape, jnp.float32)
    for position, (row_step, col_step) in enumerate(OFFSETS):
        product = coefficients[position] * values
        rows_taken = product[..., 1 - row_step : 1 - row_step + height, :]
        result = result + column_shift(rows_taken, -col_step)
    return result


def local_sums(first, second):
    return jnp.sum(first * second, axis=(1, 2, 3))


def expand(scalars):
    return scalars[:, None, None, None]


def fit_cells(totals):
    diag_first = totals[0] + RIDGE
    cross_term = totals[1]
    diag_second = totals[2] + RIDGE
    determinant = diag_first * diag_second - cross_term * cross_term
    persistence = (diag_second * totals[3] - cross_term * totals[4]) / determinant
    diffusion = (diag_first * totals[4] - cross_term * totals[3]) / determinant
    return jnp.stack([persistence, diffusion], 0)


def shards(observed, gap_mask, sea_mask, stencil, precision, noise_precision, perturbation):
    sea_float = sea_mask.astype(jnp.float32)
    coefficients = stencil.astype(jnp.float32)
    observed_precision = noise_precision * gap_mask.astype(jnp.float32)
    base_side = sea_float * observed_precision * observed
    spread = sea_float * jnp.sqrt(precision + observed_precision)
    right_sides = jnp.stack(
        [
            base_side,
            base_side + spread * perturbation[0].astype(jnp.float32),
            base_side + spread * perturbation[1].astype(jnp.float32),
        ],
        0,
    )
    static_rim = padded(coefficients, (("space", 1),), 1)
    day_number = lax.axis_index("day")
    day_total = lax.axis_size("day")

    def residual_norms(residual):
        return lax.psum(local_sums(residual, residual), ("space", "day"))

    solution = jnp.zeros_like(right_sides)
    residual = right_sides
    direction = right_sides
    norm_now = residual_norms(residual)
    for iteration in range(ITERS):
        masked = sea_float * direction
        padded_state = padded(masked, (("space", 2),), 1)
        apply_before_plane = from_behind(padded_state[:, -1:], "day", 1)
        apply_earlier = jnp.concatenate([apply_before_plane, padded_state[:, :-1]], 1)
        innovation = masked - forward_rows(apply_earlier, coefficients)
        weighted = precision * innovation
        weighted_padded = padded(weighted, (("space", 2),), 1)
        after_plane = from_behind(weighted_padded[:, :1], "day", -1)
        following = jnp.concatenate([weighted_padded[:, 1:], after_plane], 1)
        applied = weighted - transposed_rows(following, static_rim) + observed_precision * masked
        applied = sea_float * applied + (1.0 - sea_float) * direction
        curvature = lax.psum(local_sums(direction, applied), ("space", "day"))
        step_size = norm_now / curvature
        solution = solution + expand(step_size) * direction
        residual = residual - expand(step_size) * applied
        if iteration + 1 < ITERS:
            norm_next = residual_norms(residual)
            direction = residual + expand(norm_next / norm_now) * direction
            norm_now = norm_next
    samples = solution[1:]
    sample_padded = padded(samples, (("space", 2),), 1)
    before_plane = from_behind(sample_padded[:, -1:], "day", 1)
    earlier = jnp.concatenate([before_plane, sample_padded[:, :-1]], 1)
    centre = earlier[:, :, 1:-1]
    height = centre.shape[2]
    laplacian = -8.0 * centre
    for row_step, col_step in OFFSETS:
        if row_step != 0 or col_step != 0:
            laplacian = laplacian + column_shift(
                earlier[:, :, 1 + row_step : 1 + row_step + height], col_step
            )
    stacked = jnp.stack(
        [
            jnp.sum(centre * centre, axis=(0, 1)),
            jnp.sum(centre * laplacian, axis=(0, 1)),
            jnp.sum(laplacian * laplacian, axis=(0, 1)),
            jnp.sum(centre * samples, axis=(0, 1)),
            jnp.sum(laplacian * samples, axis=(0, 1)),
        ],
        0,
    )
    totals = lax.psum(stacked, "day")
    breadth = totals.shape[2] // day_total
    totals = lax.dynamic_slice_in_dim(totals, day_number * breadth, breadth, 2)
    return (solution[0], fit_cells(totals))


def solution(mesh):
    placed = (
        P("day", ("region", "space"), None),
        P("day", ("region", "space"), None),
        P(("region", "space"), None),
        P(None, ("region", "space"), None),
        P(("region", "space"), None),
        P(("region", "space"), None),
        P(None, "day", ("region", "space"), None),
    )
    return jax.shard_map(
        shards,
        mesh=mesh,
        in_specs=placed,
        out_specs=(P("day", ("region", "space"), None), P(None, ("region", "space"), "day")),
        check_vma=False,
    )
```

profile of v0, /device:TPU:0, one launch (start us, length us, event | category | flops | bytes accessed | tf_op | source)
XLA Modules:
  0.0 208.1 jit_solution(12920346424859504822)
XLA Ops:
  7.3 1.5 fusion.136
  8.8 1.3 collective-permute-start.4
  10.2 5.5 %collective-permute-start.3 = (f32[9,1,4096]{2,0,1:T(8,128)S(1)}, f32[9,1,4096]{2,0,1:T(8,128)S(1)}, u32[]{:S(2)}, u32[]{:S(2)}) collective-permute-start(f32[9,1,4096]{2,0,1:T(8,128)S(1)} %copy.10), channel_id=1, source_target_pairs={{0,2},{2,4},{4,6},{6,8},{8,10},{10,12},{12,14},{1,3},{3,5},{5,7},{... | collective-permute-start | bytes 442376 | tf_op jit(solution)/shard_map/ppermute | solution.py:18
  16.3 4.8 %collective-permute-start = (f32[3,2,1,4096]{3,2,1,0:T(1,128)S(1)}, f32[3,2,1,4096]{3,2,1,0:T(1,128)S(1)}, u32[]{:S(2)}, u32[]{:S(2)}) collective-permute-start(f32[3,2,1,4096]{3,2,1,0:T(1,128)S(1)} %get-tuple-element.83), channel_id=1, source_target_pairs={{0,2},{2,4},{4,6},{6,8},{8,10},{10,12},{12,14},{1,3},{3,5},{5,7},{... | collective-permute-start | bytes 294920 | tf_op jit(solution)/shard_map/ppermute | solution.py:18
  21.2 1.3 collective-permute-start.1
  22.6 7.4 %collective-permute-done = f32[3,2,1,4096]{3,2,1,0:T(1,128)S(1)} collective-permute-done((f32[3,2,1,4096]{3,2,1,0:T(1,128)S(1)}, f32[3,2,1,4096]{3,2,1,0:T(1,128)S(1)}, u32[]{:S(2)}, u32[]{:S(2)}) %collective-permute-start) | collective-permute-done | bytes 98336 | tf_op jit(solution)/shard_map/ppermute | solution.py:18
  30.3 1.9 collective-permute-start.2
  35.6 4.4 %collective-permute-start.5 = (f32[3,2,1,4096]{3,2,1,0:T(1,128)S(1)}, f32[3,2,1,4096]{3,2,1,0:T(1,128)S(1)}, u32[]{:S(2)}, u32[]{:S(2)}) collective-permute-start(f32[3,2,1,4096]{3,2,1,0:T(1,128)S(1)} %get-tuple-element.81), channel_id=1, source_target_pairs={{0,2},{2,4},{4,6},{6,8},{8,10},{10,12},{12,14},{1,3},{3,5},{5,7},{... | collective-permute-start | bytes 294920 | tf_op jit(solution)/shard_map/ppermute | solution.py:18
  40.0 1.3 collective-permute-start.6
  42.5 4.1 %collective-permute-done.6 = f32[3,2,1,4096]{3,2,1,0:T(1,128)S(1)} collective-permute-done((f32[3,2,1,4096]{3,2,1,0:T(1,128)S(1)}, f32[3,2,1,4096]{3,2,1,0:T(1,128)S(1)}, u32[]{:S(2)}, u32[]{:S(2)}) %collective-permute-start.6) | collective-permute-done | bytes 98336 | tf_op jit(solution)/shard_map/ppermute | solution.py:19
  47.0 1.3 collective-permute-start.7
  48.8 1.8 collective-permute-done.7
  52.6 30.4 %all-reduce.30 = (f32[3]{0:T(128)S(1)}, f32[3]{0:T(128)S(1)}) all-reduce(f32[3]{0:T(128)S(1)} %get-tuple-element.6, f32[3]{0:T(128)S(1)} %get-tuple-element.5), channel_id=1, replica_groups=mesh['region'=2,'space'=8,'day'=2] {'space','day'}, use_global_device_ids=true, to_apply=%region_1.0 | all-reduce | flops 6 | bytes 48 | tf_op jit(solution)/shard_map/psum | solution.py:95
  83.3 29.5 %psum.37 = f32[3]{0:T(128)S(1)} all-reduce(f32[3]{0:T(128)S(1)} %multiply_reduce_fusion), channel_id=1, replica_groups=mesh['region'=2,'space'=8,'day'=2] {'space','day'}, use_global_device_ids=true, to_apply=%region_5.0 | all-reduce | flops 3 | bytes 24 | tf_op jit(solution)/shard_map/psum | solution.py:95
  113.2 1.3 collective-permute-start.8
  114.5 1.3 collective-permute-start.9
  115.8 3.1 %collective-permute-done.8 = f32[3,2,1,4096]{3,2,1,0:T(1,128)S(1)} collective-permute-done((f32[3,2,1,4096]{3,2,1,0:T(1,128)S(1)}, f32[3,2,1,4096]{3,2,1,0:T(1,128)S(1)}, u32[]{:S(2)}, u32[]{:S(2)}) %collective-permute-start.8) | collective-permute-done | bytes 98336 | tf_op jit(solution)/shard_map/ppermute | solution.py:18
  119.0 2.1 collective-permute-done.9
  121.4 1.3 collective-permute-start.10
  122.7 1.3 collective-permute-done.10
  126.0 2.7 %collective-permute-start.11 = (f32[3,2,1,4096]{3,2,1,0:T(1,128)S(1)}, f32[3,2,1,4096]{3,2,1,0:T(1,128)S(1)}, u32[]{:S(2)}, u32[]{:S(2)}) collective-permute-start(f32[3,2,1,4096]{3,2,1,0:T(1,128)S(1)} %get-tuple-element.77), channel_id=1, source_target_pairs={{0,2},{2,4},{4,6},{6,8},{8,10},{10,12},{12,14},{1,3},{3,5},{5,7},{... | collective-permute-start | bytes 294920 | tf_op jit(solution)/shard_map/ppermute | solution.py:18
  128.7 1.3 collective-permute-start.12
  131.3 4.1 %collective-permute-done.12 = f32[3,2,1,4096]{3,2,1,0:T(1,128)S(1)} collective-permute-done((f32[3,2,1,4096]{3,2,1,0:T(1,128)S(1)}, f32[3,2,1,4096]{3,2,1,0:T(1,128)S(1)}, u32[]{:S(2)}, u32[]{:S(2)}) %collective-permute-start.12) | collective-permute-done | bytes 98336 | tf_op jit(solution)/shard_map/ppermute | solution.py:19
  135.7 1.5 collective-permute-start.13
  137.2 2.1 %collective-permute-done.13 = f32[3,1,6,4096]{3,2,1,0:T(8,128)S(1)} collective-permute-done((f32[3,1,6,4096]{3,2,1,0:T(8,128)S(1)}, f32[3,1,6,4096]{3,2,1,0:T(8,128)S(1)}, u32[]{:S(2)}, u32[]{:S(2)}) %collective-permute-start.13) | collective-permute-done | bytes 294944 | tf_op jit(solution)/shard_map/ppermute | solution.py:27
  141.2 29.7 %psum.38 = f32[3]{0:T(128)S(1)} all-reduce(f32[3]{0:T(128)S(1)} %fusion.103), channel_id=1, replica_groups=mesh['region'=2,'space'=8,'day'=2] {'space','day'}, use_global_device_ids=true, to_apply=%region_7.0 | all-reduce | flops 3 | bytes 24 | tf_op jit(solution)/shard_map/psum | solution.py:113
  171.2 1.3 collective-permute-start.14
  172.5 1.3 collective-permute-start.15
  173.8 1.5 collective-permute-done.14
  175.4 3.3 %collective-permute-done.15 = f32[2,2,1,4096]{3,2,1,0:T(1,128)S(1)} collective-permute-done((f32[2,2,1,4096]{3,2,1,0:T(1,128)S(1)}, f32[2,2,1,4096]{3,2,1,0:T(1,128)S(1)}, u32[]{:S(2)}, u32[]{:S(2)}) %collective-permute-start.15) | collective-permute-done | bytes 65568 | tf_op jit(solution)/shard_map/ppermute | solution.py:19
  178.9 1.3 collective-permute-start.16
  184.3 15.5 %all-reduce.33.cloned.1.call-done = f32[5,4,4096]{2,1,0:T(4,128)} async-done(((f32[5,4,4096]{2,1,0:T(4,128)}), f32[5,4,4096]{2,1,0:T(4,128)}) %all-reduce.33.cloned.1.call-update) | async-done | bytes 327696 | tf_op jit(solution)/shard_map/psum | solution.py:143
  (88 shorter events, 20.8 us)
Async XLA Ops:
  7.2 8.6 %copy-start.4 = (s32[4,4096]{1,0:T(4,128)S(1)}, s32[4,4096]{1,0:T(4,128)}, u32[]{:S(2)}) copy-start(s32[4,4096]{1,0:T(4,128)} %param.9) | copy-start | bytes 196612
  7.2 8.6 %copy-start.2 = (f32[2,4,4096]{2,1,0:T(4,128)S(1)}, f32[2,4,4096]{2,1,0:T(4,128)}, u32[]{:S(2)}) copy-start(f32[2,4,4096]{2,1,0:T(4,128)} %param.7) | copy-start | bytes 393220
  7.2 8.6 %copy-start.7 = (f32[4,4096]{1,0:T(4,128)S(1)}, f32[4,4096]{1,0:T(4,128)}, u32[]{:S(2)}) copy-start(f32[4,4096]{1,0:T(4,128)} %param.12) | copy-start | bytes 196612
  7.2 8.6 %copy-start.5 = (s32[2,4,4096]{2,1,0:T(4,128)S(1)}, s32[2,4,4096]{2,1,0:T(4,128)}, u32[]{:S(2)}) copy-start(s32[2,4,4096]{2,1,0:T(4,128)} %param.8) | copy-start | bytes 393220
  7.2 8.7 %copy-start.1 = (f32[4,4096]{1,0:T(4,128)S(1)}, f32[4,4096]{1,0:T(4,128)}, u32[]{:S(2)}) copy-start(f32[4,4096]{1,0:T(4,128)} %param.11) | copy-start | bytes 196612
  7.2 8.7 %copy-start.6 = (bf16[2,2,4,4096]{3,2,1,0:T(4,128)(2,1)S(1)}, bf16[2,2,4,4096]{3,2,1,0:T(4,128)(2,1)}, u32[]{:S(2)}) copy-start(bf16[2,2,4,4096]{3,2,1,0:T(4,128)(2,1)} %param.13) | copy-start | bytes 393220
  7.2 192.5 %all-reduce.33.cloned.1.call-start = ((), (), s32[]{:S(2)}) async-start(), calls=%async_computation | async-start | bytes 655360 | tf_op jit(solution)/shard_map/psum | solution.py:143
  8.8 23.4 %collective-permute-start.4 = (f32[9,1,4096]{2,0,1:T(8,128)S(1)}, f32[9,1,4096]{2,0,1:T(8,128)S(1)}, u32[]{:S(2)}, u32[]{:S(2)}) collective-permute-start(f32[9,1,4096]{2,0,1:T(8,128)S(1)} %copy.11), channel_id=1, source_target_pairs={{2,0},{4,2},{6,4},{8,6},{10,8},{12,10},{14,12},{3,1},{5,3},{7,5},{... | collective-permute-start | bytes 442376 | tf_op jit(solution)/shard_map/ppermute | solution.py:19
  10.2 22.2 %collective-permute-start.3 = (f32[9,1,4096]{2,0,1:T(8,128)S(1)}, f32[9,1,4096]{2,0,1:T(8,128)S(1)}, u32[]{:S(2)}, u32[]{:S(2)}) collective-permute-start(f32[9,1,4096]{2,0,1:T(8,128)S(1)} %copy.10), channel_id=1, source_target_pairs={{0,2},{2,4},{4,6},{6,8},{8,10},{10,12},{12,14},{1,3},{3,5},{5,7},{... | collective-permute-start | bytes 442376 | tf_op jit(solution)/shard_map/ppermute | solution.py:18
  15.9 6.6 %copy-start = (bf16[9,4,4096]{2,1,0:T(4,128)(2,1)S(1)}, bf16[9,4,4096]{2,1,0:T(4,128)(2,1)}, u32[]{:S(2)}) copy-start(bf16[9,4,4096]{2,1,0:T(4,128)(2,1)} %param.10) | copy-start | bytes 884740
  16.3 13.6 %collective-permute-start = (f32[3,2,1,4096]{3,2,1,0:T(1,128)S(1)}, f32[3,2,1,4096]{3,2,1,0:T(1,128)S(1)}, u32[]{:S(2)}, u32[]{:S(2)}) collective-permute-start(f32[3,2,1,4096]{3,2,1,0:T(1,128)S(1)} %get-tuple-element.83), channel_id=1, source_target_pairs={{0,2},{2,4},{4,6},{6,8},{8,10},{10,12},{12,14},{1,3},{3,5},{5,7},{... | collective-permute-start | bytes 294920 | tf_op jit(solution)/shard_map/ppermute | solution.py:18
  21.2 8.8 %collective-permute-start.1 = (f32[3,2,1,4096]{3,2,1,0:T(1,128)S(1)}, f32[3,2,1,4096]{3,2,1,0:T(1,128)S(1)}, u32[]{:S(2)}, u32[]{:S(2)}) collective-permute-start(f32[3,2,1,4096]{3,2,1,0:T(1,128)S(1)} %get-tuple-element.84), channel_id=1, source_target_pairs={{2,0},{4,2},{6,4},{8,6},{10,8},{12,10},{14,12},{3,1},{5,3},{7,5},{... | collective-permute-start | bytes 294920 | tf_op jit(solution)/shard_map/ppermute | solution.py:19
  30.3 3.3 %collective-permute-start.2 = (f32[3,1,6,4096]{3,2,1,0:T(8,128)S(1)}, f32[3,1,6,4096]{3,2,1,0:T(8,128)S(1)}, u32[]{:S(2)}, u32[]{:S(2)}) collective-permute-start(f32[3,1,6,4096]{3,2,1,0:T(8,128)S(1)} %get-tuple-element.56), channel_id=1, source_target_pairs={{0,1},{2,3},{4,5},{6,7},{8,9},{10,11},{12,13},{14,15},{16,17},{18,... | collective-permute-start | bytes 884744 | tf_op jit(solution)/shard_map/ppermute | solution.py:27
  35.6 7.0 %collective-permute-start.5 = (f32[3,2,1,4096]{3,2,1,0:T(1,128)S(1)}, f32[3,2,1,4096]{3,2,1,0:T(1,128)S(1)}, u32[]{:S(2)}, u32[]{:S(2)}) collective-permute-start(f32[3,2,1,4096]{3,2,1,0:T(1,128)S(1)} %get-tuple-element.81), channel_id=1, source_target_pairs={{0,2},{2,4},{4,6},{6,8},{8,10},{10,12},{12,14},{1,3},{3,5},{5,7},{... | collective-permute-start | bytes 294920 | tf_op jit(solution)/shard_map/ppermute | solution.py:18
  40.0 6.7 %collective-permute-start.6 = (f32[3,2,1,4096]{3,2,1,0:T(1,128)S(1)}, f32[3,2,1,4096]{3,2,1,0:T(1,128)S(1)}, u32[]{:S(2)}, u32[]{:S(2)}) collective-permute-start(f32[3,2,1,4096]{3,2,1,0:T(1,128)S(1)} %get-tuple-element.82), channel_id=1, source_target_pairs={{2,0},{4,2},{6,4},{8,6},{10,8},{12,10},{14,12},{3,1},{5,3},{7,5},{... | collective-permute-start | bytes 294920 | tf_op jit(solution)/shard_map/ppermute | solution.py:19
  47.0 3.6 %collective-permute-start.7 = (f32[3,1,6,4096]{3,2,1,0:T(8,128)S(1)}, f32[3,1,6,4096]{3,2,1,0:T(8,128)S(1)}, u32[]{:S(2)}, u32[]{:S(2)}) collective-permute-start(f32[3,1,6,4096]{3,2,1,0:T(8,128)S(1)} %get-tuple-element.49), channel_id=1, source_target_pairs={{1,0},{3,2},{5,4},{7,6},{9,8},{11,10},{13,12},{15,14},{17,16},{19,... | collective-permute-start | bytes 884744 | tf_op jit(solution)/shard_map/ppermute | solution.py:27
  113.2 5.7 %collective-permute-start.8 = (f32[3,2,1,4096]{3,2,1,0:T(1,128)S(1)}, f32[3,2,1,4096]{3,2,1,0:T(1,128)S(1)}, u32[]{:S(2)}, u32[]{:S(2)}) collective-permute-start(f32[3,2,1,4096]{3,2,1,0:T(1,128)S(1)} %get-tuple-element.79), channel_id=1, source_target_pairs={{0,2},{2,4},{4,6},{6,8},{8,10},{10,12},{12,14},{1,3},{3,5},{5,7},{... | collective-permute-start | bytes 294920 | tf_op jit(solution)/shard_map/ppermute | solution.py:18
  114.5 6.5 %collective-permute-start.9 = (f32[3,2,1,4096]{3,2,1,0:T(1,128)S(1)}, f32[3,2,1,4096]{3,2,1,0:T(1,128)S(1)}, u32[]{:S(2)}, u32[]{:S(2)}) collective-permute-start(f32[3,2,1,4096]{3,2,1,0:T(1,128)S(1)} %get-tuple-element.80), channel_id=1, source_target_pairs={{2,0},{4,2},{6,4},{8,6},{10,8},{12,10},{14,12},{3,1},{5,3},{7,5},{... | collective-permute-start | bytes 294920 | tf_op jit(solution)/shard_map/ppermute | solution.py:19
  121.4 2.6 %collective-permute-start.10 = (f32[3,1,6,4096]{3,2,1,0:T(8,128)S(1)}, f32[3,1,6,4096]{3,2,1,0:T(8,128)S(1)}, u32[]{:S(2)}, u32[]{:S(2)}) collective-permute-start(f32[3,1,6,4096]{3,2,1,0:T(8,128)S(1)} %get-tuple-element.41), channel_id=1, source_target_pairs={{0,1},{2,3},{4,5},{6,7},{8,9},{10,11},{12,13},{14,15},{16,17},{18,... | collective-permute-start | bytes 884744 | tf_op jit(solution)/shard_map/ppermute | solution.py:27
  126.0 5.3 %collective-permute-start.11 = (f32[3,2,1,4096]{3,2,1,0:T(1,128)S(1)}, f32[3,2,1,4096]{3,2,1,0:T(1,128)S(1)}, u32[]{:S(2)}, u32[]{:S(2)}) collective-permute-start(f32[3,2,1,4096]{3,2,1,0:T(1,128)S(1)} %get-tuple-element.77), channel_id=1, source_target_pairs={{0,2},{2,4},{4,6},{6,8},{8,10},{10,12},{12,14},{1,3},{3,5},{5,7},{... | collective-permute-start | bytes 294920 | tf_op jit(solution)/shard_map/ppermute | solution.py:18
  128.7 6.7 %collective-permute-start.12 = (f32[3,2,1,4096]{3,2,1,0:T(1,128)S(1)}, f32[3,2,1,4096]{3,2,1,0:T(1,128)S(1)}, u32[]{:S(2)}, u32[]{:S(2)}) collective-permute-start(f32[3,2,1,4096]{3,2,1,0:T(1,128)S(1)} %get-tuple-element.78), channel_id=1, source_target_pairs={{2,0},{4,2},{6,4},{8,6},{10,8},{12,10},{14,12},{3,1},{5,3},{7,5},{... | collective-permute-start | bytes 294920 | tf_op jit(solution)/shard_map/ppermute | solution.py:19
  135.7 3.6 %collective-permute-start.13 = (f32[3,1,6,4096]{3,2,1,0:T(8,128)S(1)}, f32[3,1,6,4096]{3,2,1,0:T(8,128)S(1)}, u32[]{:S(2)}, u32[]{:S(2)}) collective-permute-start(f32[3,1,6,4096]{3,2,1,0:T(8,128)S(1)} %get-tuple-element.34), channel_id=1, source_target_pairs={{1,0},{3,2},{5,4},{7,6},{9,8},{11,10},{13,12},{15,14},{17,16},{19,... | collective-permute-start | bytes 884744 | tf_op jit(solution)/shard_map/ppermute | solution.py:27
  171.2 4.1 %collective-permute-start.14 = (f32[2,2,1,4096]{3,2,1,0:T(1,128)S(1)}, f32[2,2,1,4096]{3,2,1,0:T(1,128)S(1)}, u32[]{:S(2)}, u32[]{:S(2)}) collective-permute-start(f32[2,2,1,4096]{3,2,1,0:T(1,128)S(1)} %get-tuple-element.75), channel_id=1, source_target_pairs={{0,2},{2,4},{4,6},{6,8},{8,10},{10,12},{12,14},{1,3},{3,5},{5,7},{... | collective-permute-start | bytes 196616 | tf_op jit(solution)/shard_map/ppermute | solution.py:18
  172.5 6.2 %collective-permute-start.15 = (f32[2,2,1,4096]{3,2,1,0:T(1,128)S(1)}, f32[2,2,1,4096]{3,2,1,0:T(1,128)S(1)}, u32[]{:S(2)}, u32[]{:S(2)}) collective-permute-start(f32[2,2,1,4096]{3,2,1,0:T(1,128)S(1)} %get-tuple-element.76), channel_id=1, source_target_pairs={{2,0},{4,2},{6,4},{8,6},{10,8},{12,10},{14,12},{3,1},{5,3},{7,5},{... | collective-permute-start | bytes 196616 | tf_op jit(solution)/shard_map/ppermute | solution.py:19
  178.9 2.4 %collective-permute-start.16 = (f32[2,1,6,4096]{3,2,1,0:T(8,128)S(1)}, f32[2,1,6,4096]{3,2,1,0:T(8,128)S(1)}, u32[]{:S(2)}, u32[]{:S(2)}) collective-permute-start(f32[2,1,6,4096]{3,2,1,0:T(8,128)S(1)} %get-tuple-element.72), channel_id=1, source_target_pairs={{0,1},{2,3},{4,5},{6,7},{8,9},{10,11},{12,13},{14,15},{16,17},{18,... | collective-permute-start | bytes 589832 | tf_op jit(solution)/shard_map/ppermute | solution.py:27
  182.8 0.7 copy-start.3
Sparse Core Ops, SparseCore 0:
  183.7 15.9 all-reduce.32
where the time goes:
time: 209 us; the launch traced here: 208 us
  blocking collectives  89.6 us (43%)
  waiting for transfers between devices  50.6 us (24%)
  starting transfers between devices  35.2 us (17%)
  between operations  14.7 us (7%)
  other arithmetic  13.1 us (6%)
  local copies, waits for them, and re-layouts  4.99 us (2%)
    psum x2, blocking collectives, residual_norms(): return lax.psum(local_sums(residual, residual), ('space', 'day'))  59.9 us
    psum x1, blocking collectives, shards(): curvature = lax.psum(local_sums(direction, applied), ('space', 'day'))  29.7 us
    ppermute x6, starting transfers between devices, padded(): before = lax.ppermute(last, axis, up)  20 us
    psum x1, waiting for transfers between devices, shards(): totals = lax.psum(stacked, 'day')  15.5 us
    ppermute x6, waiting for transfers between devices, padded(): before = lax.ppermute(last, axis, up)  14.2 us
    ppermute x6, waiting for transfers between devices, padded(): after = lax.ppermute(first, axis, down)  13.6 us
    ppermute x6, starting transfers between devices, padded(): after = lax.ppermute(first, axis, down)  7.75 us
    ppermute x5, starting transfers between devices, from_behind(): return lax.ppermute(x, axis, pairs)  7.33 us
  transfers between devices with their start and end apart: 18, of which 15 were waited for; matrix products, arithmetic and copies ran while one was open for 1% of the time, Pallas kernels for 0%

commit v1 on v0

--- a/solution.py
+++ b/solution.py
@@ -92,7 +92,7 @@
     day_total = lax.axis_size("day")
 
     def residual_norms(residual):
-        return lax.psum(local_sums(residual, residual), ("space", "day"))
+        return lax.psum(lax.psum(local_sums(residual, residual), "day"), "space")
 
     solution = jnp.zeros_like(right_sides)
     residual = right_sides

time: 209 us -> 221 us (1.057)
  blocking collectives: 89.6 us -> 101 us
    psum x1 -> x2, blocking collectives: 29.7 us -> 60.1 us  [shards(): curvature = lax.psum(local_sums(direction, applied), ('space', 'day'))]
    psum x2 -> x4, blocking collectives: 59.9 us -> 41.1 us  [residual_norms(): return lax.psum(lax.psum(local_sums(residual, residual), 'day'), 'space')]
where the time goes in v1:
time: 221 us; the launch traced here: 220 us
  blocking collectives  101 us (46%)
  waiting for transfers between devices  50.5 us (23%)
  starting transfers between devices  36.1 us (16%)
  between operations  14.7 us (7%)
  other arithmetic  13.1 us (6%)
  local copies, waits for them, and re-layouts  4.98 us (2%)
    psum x2, blocking collectives, shards(): curvature = lax.psum(local_sums(direction, applied), ('space', 'day'))  60.1 us
    psum x4, blocking collectives, residual_norms(): return lax.psum(lax.psum(local_sums(residual, residual), 'day'), 'space')  41.1 us
    ppermute x6, starting transfers between devices, padded(): before = lax.ppermute(last, axis, up)  21 us
    ppermute x6, waiting for transfers between devices, padded(): after = lax.ppermute(first, axis, down)  15.8 us
    psum x1, waiting for transfers between devices, shards(): totals = lax.psum(stacked, 'day')  15.4 us
    ppermute x6, waiting for transfers between devices, padded(): before = lax.ppermute(last, axis, up)  12 us
    ppermute x6, starting transfers between devices, padded(): after = lax.ppermute(first, axis, down)  7.75 us
    ppermute x5, starting transfers between devices, from_behind(): return lax.ppermute(x, axis, pairs)  7.33 us
  transfers between devices with their start and end apart: 18, of which 15 were waited for; matrix products, arithmetic and copies ran while one was open for 1% of the time, Pallas kernels for 0%

profile of v1, /device:TPU:0, one launch (start us, length us, event | category | flops | bytes accessed | tf_op | source)
XLA Modules:
  0.0 220.5 jit_solution(10167833488906694603)
XLA Ops:
  7.3 1.5 fusion.136
  8.8 1.3 collective-permute-start.4
  10.2 5.5 %collective-permute-start.3 = (f32[9,1,4096]{2,0,1:T(8,128)S(1)}, f32[9,1,4096]{2,0,1:T(8,128)S(1)}, u32[]{:S(2)}, u32[]{:S(2)}) collective-permute-start(f32[9,1,4096]{2,0,1:T(8,128)S(1)} %copy.10), channel_id=1, source_target_pairs={{0,2},{2,4},{4,6},{6,8},{8,10},{10,12},{12,14},{1,3},{3,5},{5,7},{... | collective-permute-start | bytes 442376 | tf_op jit(solution)/shard_map/ppermute | solution.py:18
  16.3 4.8 %collective-permute-start = (f32[3,2,1,4096]{3,2,1,0:T(1,128)S(1)}, f32[3,2,1,4096]{3,2,1,0:T(1,128)S(1)}, u32[]{:S(2)}, u32[]{:S(2)}) collective-permute-start(f32[3,2,1,4096]{3,2,1,0:T(1,128)S(1)} %get-tuple-element.81), channel_id=1, source_target_pairs={{0,2},{2,4},{4,6},{6,8},{8,10},{10,12},{12,14},{1,3},{3,5},{5,7},{... | collective-permute-start | bytes 294920 | tf_op jit(solution)/shard_map/ppermute | solution.py:18
  21.2 1.3 collective-permute-start.1
  22.6 7.4 %collective-permute-done = f32[3,2,1,4096]{3,2,1,0:T(1,128)S(1)} collective-permute-done((f32[3,2,1,4096]{3,2,1,0:T(1,128)S(1)}, f32[3,2,1,4096]{3,2,1,0:T(1,128)S(1)}, u32[]{:S(2)}, u32[]{:S(2)}) %collective-permute-start) | collective-permute-done | bytes 98336 | tf_op jit(solution)/shard_map/ppermute | solution.py:18
  30.3 1.9 collective-permute-start.2
  35.6 4.4 %collective-permute-start.5 = (f32[3,2,1,4096]{3,2,1,0:T(1,128)S(1)}, f32[3,2,1,4096]{3,2,1,0:T(1,128)S(1)}, u32[]{:S(2)}, u32[]{:S(2)}) collective-permute-start(f32[3,2,1,4096]{3,2,1,0:T(1,128)S(1)} %get-tuple-element.79), channel_id=1, source_target_pairs={{0,2},{2,4},{4,6},{6,8},{8,10},{10,12},{12,14},{1,3},{3,5},{5,7},{... | collective-permute-start | bytes 294920 | tf_op jit(solution)/shard_map/ppermute | solution.py:18
  40.0 1.3 collective-permute-start.6
  42.5 4.1 %collective-permute-done.6 = f32[3,2,1,4096]{3,2,1,0:T(1,128)S(1)} collective-permute-done((f32[3,2,1,4096]{3,2,1,0:T(1,128)S(1)}, f32[3,2,1,4096]{3,2,1,0:T(1,128)S(1)}, u32[]{:S(2)}, u32[]{:S(2)}) %collective-permute-start.6) | collective-permute-done | bytes 98336 | tf_op jit(solution)/shard_map/ppermute | solution.py:19
  48.8 1.8 collective-permute-done.7
  52.6 2.5 %psum.49 = f32[3]{0:T(128)S(1)} all-reduce(f32[3]{0:T(128)S(1)} %get-tuple-element.6), channel_id=1, replica_groups=mesh['region'=2,'space'=8,'day'=2] {'day'}, use_global_device_ids=true, to_apply=%region_1.0 | all-reduce | flops 3 | bytes 24 | tf_op jit(solution)/shard_map/psum | solution.py:95
  55.0 30.5 %psum.51 = f32[3]{0:T(128)S(1)} all-reduce(f32[3]{0:T(128)S(1)} %get-tuple-element.5), channel_id=1, replica_groups=mesh['region'=2,'space'=8,'day'=2] {'space','day'}, use_global_device_ids=true, to_apply=%region_4.0 | all-reduce | flops 3 | bytes 24 | tf_op jit(solution)/shard_map/psum | solution.py:113
  85.5 17.1 %psum.50 = f32[3]{0:T(128)S(1)} all-reduce(f32[3]{0:T(128)S(1)} %psum.49), channel_id=1, replica_groups=mesh['region'=2,'space'=8,'day'=2] {'space'}, use_global_device_ids=true, to_apply=%region_2.0 | all-reduce | flops 3 | bytes 24 | tf_op jit(solution)/shard_map/psum | solution.py:95
  102.9 2.4 %psum.52 = f32[3]{0:T(128)S(1)} all-reduce(f32[3]{0:T(128)S(1)} %multiply_reduce_fusion), channel_id=1, replica_groups=mesh['region'=2,'space'=8,'day'=2] {'day'}, use_global_device_ids=true, to_apply=%region_6.0 | all-reduce | flops 3 | bytes 24 | tf_op jit(solution)/shard_map/psum | solution.py:95
  105.4 19.1 %psum.53 = f32[3]{0:T(128)S(1)} all-reduce(f32[3]{0:T(128)S(1)} %psum.52), channel_id=1, replica_groups=mesh['region'=2,'space'=8,'day'=2] {'space'}, use_global_device_ids=true, to_apply=%region_7.0 | all-reduce | flops 3 | bytes 24 | tf_op jit(solution)/shard_map/psum | solution.py:95
  124.9 1.9 collective-permute-start.8
  129.0 4.3 %collective-permute-done.9 = f32[3,2,1,4096]{3,2,1,0:T(1,128)S(1)} collective-permute-done((f32[3,2,1,4096]{3,2,1,0:T(1,128)S(1)}, f32[3,2,1,4096]{3,2,1,0:T(1,128)S(1)}, u32[]{:S(2)}, u32[]{:S(2)}) %collective-permute-start.9) | collective-permute-done | bytes 98336 | tf_op jit(solution)/shard_map/ppermute | solution.py:19
  133.7 1.3 collective-permute-start.10
  135.0 1.3 collective-permute-done.10
  138.3 3.0 %collective-permute-start.11 = (f32[3,2,1,4096]{3,2,1,0:T(1,128)S(1)}, f32[3,2,1,4096]{3,2,1,0:T(1,128)S(1)}, u32[]{:S(2)}, u32[]{:S(2)}) collective-permute-start(f32[3,2,1,4096]{3,2,1,0:T(1,128)S(1)} %get-tuple-element.75), channel_id=1, source_target_pairs={{0,2},{2,4},{4,6},{6,8},{8,10},{10,12},{12,14},{1,3},{3,5},{5,7},{... | collective-permute-start | bytes 294920 | tf_op jit(solution)/shard_map/ppermute | solution.py:18
  141.3 1.3 collective-permute-start.12
  143.9 4.1 %collective-permute-done.12 = f32[3,2,1,4096]{3,2,1,0:T(1,128)S(1)} collective-permute-done((f32[3,2,1,4096]{3,2,1,0:T(1,128)S(1)}, f32[3,2,1,4096]{3,2,1,0:T(1,128)S(1)}, u32[]{:S(2)}, u32[]{:S(2)}) %collective-permute-start.12) | collective-permute-done | bytes 98336 | tf_op jit(solution)/shard_map/ppermute | solution.py:19
  148.3 1.5 collective-permute-start.13
  149.8 2.1 collective-permute-done.13
  153.8 29.6 %psum.54 = f32[3]{0:T(128)S(1)} all-reduce(f32[3]{0:T(128)S(1)} %fusion.103), channel_id=1, replica_groups=mesh['region'=2,'space'=8,'day'=2] {'space','day'}, use_global_device_ids=true, to_apply=%region_9.0 | all-reduce | flops 3 | bytes 24 | tf_op jit(solution)/shard_map/psum | solution.py:113
  183.7 1.3 collective-permute-start.14
  185.0 1.3 collective-permute-start.15
  186.3 1.6 collective-permute-done.14
  188.0 3.2 %collective-permute-done.15 = f32[2,2,1,4096]{3,2,1,0:T(1,128)S(1)} collective-permute-done((f32[2,2,1,4096]{3,2,1,0:T(1,128)S(1)}, f32[2,2,1,4096]{3,2,1,0:T(1,128)S(1)}, u32[]{:S(2)}, u32[]{:S(2)}) %collective-permute-start.15) | collective-permute-done | bytes 65568 | tf_op jit(solution)/shard_map/ppermute | solution.py:19
  191.4 1.3 collective-permute-start.16
  196.8 15.4 %all-reduce.32.cloned.1.call-done = f32[5,4,4096]{2,1,0:T(4,128)} async-done(((f32[5,4,4096]{2,1,0:T(4,128)}), f32[5,4,4096]{2,1,0:T(4,128)}) %all-reduce.32.cloned.1.call-update) | async-done | bytes 327696 | tf_op jit(solution)/shard_map/psum | solution.py:143
  (91 shorter events, 24.3 us)
Async XLA Ops:
  7.2 8.6 %copy-start.4 = (s32[4,4096]{1,0:T(4,128)S(1)}, s32[4,4096]{1,0:T(4,128)}, u32[]{:S(2)}) copy-start(s32[4,4096]{1,0:T(4,128)} %param.9) | copy-start | bytes 196612
  7.2 8.6 %copy-start.2 = (f32[2,4,4096]{2,1,0:T(4,128)S(1)}, f32[2,4,4096]{2,1,0:T(4,128)}, u32[]{:S(2)}) copy-start(f32[2,4,4096]{2,1,0:T(4,128)} %param.7) | copy-start | bytes 393220
  7.2 8.6 %copy-start.7 = (f32[4,4096]{1,0:T(4,128)S(1)}, f32[4,4096]{1,0:T(4,128)}, u32[]{:S(2)}) copy-start(f32[4,4096]{1,0:T(4,128)} %param.12) | copy-start | bytes 196612
  7.2 8.6 %copy-start.5 = (s32[2,4,4096]{2,1,0:T(4,128)S(1)}, s32[2,4,4096]{2,1,0:T(4,128)}, u32[]{:S(2)}) copy-start(s32[2,4,4096]{2,1,0:T(4,128)} %param.8) | copy-start | bytes 393220
  7.2 8.7 %copy-start.1 = (f32[4,4096]{1,0:T(4,128)S(1)}, f32[4,4096]{1,0:T(4,128)}, u32[]{:S(2)}) copy-start(f32[4,4096]{1,0:T(4,128)} %param.11) | copy-start | bytes 196612
  7.2 8.7 %copy-start.6 = (bf16[2,2,4,4096]{3,2,1,0:T(4,128)(2,1)S(1)}, bf16[2,2,4,4096]{3,2,1,0:T(4,128)(2,1)}, u32[]{:S(2)}) copy-start(bf16[2,2,4,4096]{3,2,1,0:T(4,128)(2,1)} %param.13) | copy-start | bytes 393220
  7.2 204.9 %all-reduce.32.cloned.1.call-start = ((), (), s32[]{:S(2)}) async-start(), calls=%async_computation | async-start | bytes 655360 | tf_op jit(solution)/shard_map/psum | solution.py:143
  8.8 23.4 %collective-permute-start.4 = (f32[9,1,4096]{2,0,1:T(8,128)S(1)}, f32[9,1,4096]{2,0,1:T(8,128)S(1)}, u32[]{:S(2)}, u32[]{:S(2)}) collective-permute-start(f32[9,1,4096]{2,0,1:T(8,128)S(1)} %copy.11), channel_id=1, source_target_pairs={{2,0},{4,2},{6,4},{8,6},{10,8},{12,10},{14,12},{3,1},{5,3},{7,5},{... | collective-permute-start | bytes 442376 | tf_op jit(solution)/shard_map/ppermute | solution.py:19
  10.2 22.2 %collective-permute-start.3 = (f32[9,1,4096]{2,0,1:T(8,128)S(1)}, f32[9,1,4096]{2,0,1:T(8,128)S(1)}, u32[]{:S(2)}, u32[]{:S(2)}) collective-permute-start(f32[9,1,4096]{2,0,1:T(8,128)S(1)} %copy.10), channel_id=1, source_target_pairs={{0,2},{2,4},{4,6},{6,8},{8,10},{10,12},{12,14},{1,3},{3,5},{5,7},{... | collective-permute-start | bytes 442376 | tf_op jit(solution)/shard_map/ppermute | solution.py:18
  15.9 6.6 %copy-start = (bf16[9,4,4096]{2,1,0:T(4,128)(2,1)S(1)}, bf16[9,4,4096]{2,1,0:T(4,128)(2,1)}, u32[]{:S(2)}) copy-start(bf16[9,4,4096]{2,1,0:T(4,128)(2,1)} %param.10) | copy-start | bytes 884740
  16.3 13.6 %collective-permute-start = (f32[3,2,1,4096]{3,2,1,0:T(1,128)S(1)}, f32[3,2,1,4096]{3,2,1,0:T(1,128)S(1)}, u32[]{:S(2)}, u32[]{:S(2)}) collective-permute-start(f32[3,2,1,4096]{3,2,1,0:T(1,128)S(1)} %get-tuple-element.81), channel_id=1, source_target_pairs={{0,2},{2,4},{4,6},{6,8},{8,10},{10,12},{12,14},{1,3},{3,5},{5,7},{... | collective-permute-start | bytes 294920 | tf_op jit(solution)/shard_map/ppermute | solution.py:18
  21.2 8.8 %collective-permute-start.1 = (f32[3,2,1,4096]{3,2,1,0:T(1,128)S(1)}, f32[3,2,1,4096]{3,2,1,0:T(1,128)S(1)}, u32[]{:S(2)}, u32[]{:S(2)}) collective-permute-start(f32[3,2,1,4096]{3,2,1,0:T(1,128)S(1)} %get-tuple-element.82), channel_id=1, source_target_pairs={{2,0},{4,2},{6,4},{8,6},{10,8},{12,10},{14,12},{3,1},{5,3},{7,5},{... | collective-permute-start | bytes 294920 | tf_op jit(solution)/shard_map/ppermute | solution.py:19
  30.3 3.3 %collective-permute-start.2 = (f32[3,1,6,4096]{3,2,1,0:T(8,128)S(1)}, f32[3,1,6,4096]{3,2,1,0:T(8,128)S(1)}, u32[]{:S(2)}, u32[]{:S(2)}) collective-permute-start(f32[3,1,6,4096]{3,2,1,0:T(8,128)S(1)} %get-tuple-element.54), channel_id=1, source_target_pairs={{0,1},{2,3},{4,5},{6,7},{8,9},{10,11},{12,13},{14,15},{16,17},{18,... | collective-permute-start | bytes 884744 | tf_op jit(solution)/shard_map/ppermute | solution.py:27
  35.6 7.0 %collective-permute-start.5 = (f32[3,2,1,4096]{3,2,1,0:T(1,128)S(1)}, f32[3,2,1,4096]{3,2,1,0:T(1,128)S(1)}, u32[]{:S(2)}, u32[]{:S(2)}) collective-permute-start(f32[3,2,1,4096]{3,2,1,0:T(1,128)S(1)} %get-tuple-element.79), channel_id=1, source_target_pairs={{0,2},{2,4},{4,6},{6,8},{8,10},{10,12},{12,14},{1,3},{3,5},{5,7},{... | collective-permute-start | bytes 294920 | tf_op jit(solution)/shard_map/ppermute | solution.py:18
  40.0 6.7 %collective-permute-start.6 = (f32[3,2,1,4096]{3,2,1,0:T(1,128)S(1)}, f32[3,2,1,4096]{3,2,1,0:T(1,128)S(1)}, u32[]{:S(2)}, u32[]{:S(2)}) collective-permute-start(f32[3,2,1,4096]{3,2,1,0:T(1,128)S(1)} %get-tuple-element.80), channel_id=1, source_target_pairs={{2,0},{4,2},{6,4},{8,6},{10,8},{12,10},{14,12},{3,1},{5,3},{7,5},{... | collective-permute-start | bytes 294920 | tf_op jit(solution)/shard_map/ppermute | solution.py:19
  47.0 3.6 %collective-permute-start.7 = (f32[3,1,6,4096]{3,2,1,0:T(8,128)S(1)}, f32[3,1,6,4096]{3,2,1,0:T(8,128)S(1)}, u32[]{:S(2)}, u32[]{:S(2)}) collective-permute-start(f32[3,1,6,4096]{3,2,1,0:T(8,128)S(1)} %get-tuple-element.47), channel_id=1, source_target_pairs={{1,0},{3,2},{5,4},{7,6},{9,8},{11,10},{13,12},{15,14},{17,16},{19,... | collective-permute-start | bytes 884744 | tf_op jit(solution)/shard_map/ppermute | solution.py:27
  124.9 4.1 %collective-permute-start.8 = (f32[3,2,1,4096]{3,2,1,0:T(1,128)S(1)}, f32[3,2,1,4096]{3,2,1,0:T(1,128)S(1)}, u32[]{:S(2)}, u32[]{:S(2)}) collective-permute-start(f32[3,2,1,4096]{3,2,1,0:T(1,128)S(1)} %get-tuple-element.77), channel_id=1, source_target_pairs={{0,2},{2,4},{4,6},{6,8},{8,10},{10,12},{12,14},{1,3},{3,5},{5,7},{... | collective-permute-start | bytes 294920 | tf_op jit(solution)/shard_map/ppermute | solution.py:18
  126.8 6.5 %collective-permute-start.9 = (f32[3,2,1,4096]{3,2,1,0:T(1,128)S(1)}, f32[3,2,1,4096]{3,2,1,0:T(1,128)S(1)}, u32[]{:S(2)}, u32[]{:S(2)}) collective-permute-start(f32[3,2,1,4096]{3,2,1,0:T(1,128)S(1)} %get-tuple-element.78), channel_id=1, source_target_pairs={{2,0},{4,2},{6,4},{8,6},{10,8},{12,10},{14,12},{3,1},{5,3},{7,5},{... | collective-permute-start | bytes 294920 | tf_op jit(solution)/shard_map/ppermute | solution.py:19
  133.7 2.6 %collective-permute-start.10 = (f32[3,1,6,4096]{3,2,1,0:T(8,128)S(1)}, f32[3,1,6,4096]{3,2,1,0:T(8,128)S(1)}, u32[]{:S(2)}, u32[]{:S(2)}) collective-permute-start(f32[3,1,6,4096]{3,2,1,0:T(8,128)S(1)} %get-tuple-element.39), channel_id=1, source_target_pairs={{0,1},{2,3},{4,5},{6,7},{8,9},{10,11},{12,13},{14,15},{16,17},{18,... | collective-permute-start | bytes 884744 | tf_op jit(solution)/shard_map/ppermute | solution.py:27
  138.3 5.6 %collective-permute-start.11 = (f32[3,2,1,4096]{3,2,1,0:T(1,128)S(1)}, f32[3,2,1,4096]{3,2,1,0:T(1,128)S(1)}, u32[]{:S(2)}, u32[]{:S(2)}) collective-permute-start(f32[3,2,1,4096]{3,2,1,0:T(1,128)S(1)} %get-tuple-element.75), channel_id=1, source_target_pairs={{0,2},{2,4},{4,6},{6,8},{8,10},{10,12},{12,14},{1,3},{3,5},{5,7},{... | collective-permute-start | bytes 294920 | tf_op jit(solution)/shard_map/ppermute | solution.py:18
  141.3 6.7 %collective-permute-start.12 = (f32[3,2,1,4096]{3,2,1,0:T(1,128)S(1)}, f32[3,2,1,4096]{3,2,1,0:T(1,128)S(1)}, u32[]{:S(2)}, u32[]{:S(2)}) collective-permute-start(f32[3,2,1,4096]{3,2,1,0:T(1,128)S(1)} %get-tuple-element.76), channel_id=1, source_target_pairs={{2,0},{4,2},{6,4},{8,6},{10,8},{12,10},{14,12},{3,1},{5,3},{7,5},{... | collective-permute-start | bytes 294920 | tf_op jit(solution)/shard_map/ppermute | solution.py:19
  148.3 3.6 %collective-permute-start.13 = (f32[3,1,6,4096]{3,2,1,0:T(8,128)S(1)}, f32[3,1,6,4096]{3,2,1,0:T(8,128)S(1)}, u32[]{:S(2)}, u32[]{:S(2)}) collective-permute-start(f32[3,1,6,4096]{3,2,1,0:T(8,128)S(1)} %get-tuple-element.32), channel_id=1, source_target_pairs={{1,0},{3,2},{5,4},{7,6},{9,8},{11,10},{13,12},{15,14},{17,16},{19,... | collective-permute-start | bytes 884744 | tf_op jit(solution)/shard_map/ppermute | solution.py:27
  183.7 4.2 %collective-permute-start.14 = (f32[2,2,1,4096]{3,2,1,0:T(1,128)S(1)}, f32[2,2,1,4096]{3,2,1,0:T(1,128)S(1)}, u32[]{:S(2)}, u32[]{:S(2)}) collective-permute-start(f32[2,2,1,4096]{3,2,1,0:T(1,128)S(1)} %get-tuple-element.73), channel_id=1, source_target_pairs={{0,2},{2,4},{4,6},{6,8},{8,10},{10,12},{12,14},{1,3},{3,5},{5,7},{... | collective-permute-start | bytes 196616 | tf_op jit(solution)/shard_map/ppermute | solution.py:18
  185.0 6.2 %collective-permute-start.15 = (f32[2,2,1,4096]{3,2,1,0:T(1,128)S(1)}, f32[2,2,1,4096]{3,2,1,0:T(1,128)S(1)}, u32[]{:S(2)}, u32[]{:S(2)}) collective-permute-start(f32[2,2,1,4096]{3,2,1,0:T(1,128)S(1)} %get-tuple-element.74), channel_id=1, source_target_pairs={{2,0},{4,2},{6,4},{8,6},{10,8},{12,10},{14,12},{3,1},{5,3},{7,5},{... | collective-permute-start | bytes 196616 | tf_op jit(solution)/shard_map/ppermute | solution.py:19
  191.4 2.4 %collective-permute-start.16 = (f32[2,1,6,4096]{3,2,1,0:T(8,128)S(1)}, f32[2,1,6,4096]{3,2,1,0:T(8,128)S(1)}, u32[]{:S(2)}, u32[]{:S(2)}) collective-permute-start(f32[2,1,6,4096]{3,2,1,0:T(8,128)S(1)} %get-tuple-element.70), channel_id=1, source_target_pairs={{0,1},{2,3},{4,5},{6,7},{8,9},{10,11},{12,13},{14,15},{16,17},{18,... | collective-permute-start | bytes 589832 | tf_op jit(solution)/shard_map/ppermute | solution.py:27
  195.3 0.7 copy-start.3
Sparse Core Ops, SparseCore 0:
  196.2 15.8 all-reduce.31
